TPU v7x, 512 devices: a whole 4x8x8 slice. The times are simulated.
512 devices in a mesh: ctx: 32 (over y, x), head: 16 (over z, core).
Axes of the slice: x: 4, y: 8, z: 8, core: 2. Of those that a mesh axis runs over, the one named last changes fastest.
Arguments:
- activations: bfloat16 [8192, 16384], P('ctx'), may hold values from -6 to 6
- w_query: bfloat16 [16384, 2048], P('ctx', 'head'), may hold values from -0.046875 to 0.046875
- w_keyval: bfloat16 [16384, 256], P('ctx', 'head'), may hold values from -0.046875 to 0.046875
- f_query: bfloat16 [16, 128, 128], P('head'), may hold values from -1 to 1
- f_key: bfloat16 [128, 128], replicated, may hold values from -1 to 1
- w_out: bfloat16 [2048, 16384], P('ctx', 'head'), may hold values from -0.75 to 0.75
Outputs:
- sublayer_out: bfloat16 [8192, 16384], P('ctx', 'head')
All inputs are finite; a program needn't handle non-finite values.
Results may differ from a plain program's by a relative error of at most 0.0086.
Values may be sent and summed in bfloat16 or wider, within the bound.
A program may use at most 64 MiB of HBM per device.

v0:
```python
import math
import jax
import jax.numpy as jnp
from jax import lax
from jax.sharding import PartitionSpec as P

WINDOW = 64


def from_behind(array, axis, by):
    size = lax.axis_size(axis)
    pairs = [(i, i + by) for i in range(size) if 0 <= i + by < size]
    return lax.ppermute(array, axis, pairs)


def prefix(array, axis, combine, identity):
    size, mine = (lax.axis_size(axis), lax.axis_index(axis))
    everything = jax.tree.map(
        lambda part, kind: lax.all_gather(part.astype(kind), axis),
        array,
        jax.tree.map(lambda a: jnp.bfloat16 if a.dtype == jnp.float32 else a.dtype, array),
    )
    start = jax.tree.map(
        lambda part, zero: jnp.broadcast_to(jnp.asarray(zero, part.dtype), part.shape),
        array,
        identity,
    )

    def step(k, before):
        reached = k < mine
        new = combine(
            before, jax.tree.map(lambda part, own: part[k].astype(own.dtype), everything, array)
        )
        return jax.tree.map(lambda a, b: jnp.where(reached, a, b), new, before)

    return lax.fori_loop(0, size, step, start)


def normalized(logits):
    rising = jnp.exp(logits)
    falling = jnp.exp(-logits)
    rising = rising / jnp.sum(rising, axis=-1, keepdims=True)
    falling = falling / jnp.sum(falling, axis=-1, keepdims=True)
    return jnp.concatenate([rising, falling], axis=-1).astype(jnp.bfloat16)


def state_of(features, values):
    matrix = jnp.einsum("nf,nc->fc", features, values, preferred_element_type=jnp.float32)
    totals = jnp.sum(features.astype(jnp.float32), axis=0)
    return (matrix, totals)


def add_states(earlier, later):
    return (earlier[0] + later[0], earlier[1] + later[1])


def per_device(activations, w_query, w_keyval, f_query, f_key, w_out):
    length = activations.shape[0]
    head_width = f_key.shape[0]
    local_heads = f_query.shape[0]
    columns = activations
    query_sum = jnp.dot(
        columns,
        lax.all_gather(w_query, "ctx", axis=0, tiled=True),
        preferred_element_type=jnp.float32,
    )
    pair_sum = jnp.dot(
        columns,
        lax.all_gather(w_keyval, "ctx", axis=0, tiled=True),
        preferred_element_type=jnp.float32,
    )
    queries = query_sum.astype(jnp.bfloat16)
    keyval = lax.all_gather(pair_sum.astype(jnp.bfloat16), "head", axis=1, tiled=True)
    border = from_behind(keyval[length - WINDOW :], "ctx", 1)
    extended = jnp.concatenate([border, keyval], axis=0)
    ext_keys = extended[:, :head_width]
    ext_vals = extended[:, head_width:]
    first_pos = lax.axis_index("ctx") * length - WINDOW
    present = first_pos + jnp.arange(length + WINDOW) >= 0
    ext_feats = normalized(jnp.dot(ext_keys, f_key, preferred_element_type=jnp.float32))
    ext_feats = jnp.where(present[:, None], ext_feats, jnp.zeros_like(ext_feats))
    contribution = state_of(ext_feats[:length], ext_vals[:length])
    identity = (
        jnp.zeros((2 * head_width, head_width), jnp.float32),
        jnp.zeros((2 * head_width,), jnp.float32),
    )
    matrix, totals = prefix(contribution, "ctx", add_states, identity)
    query_heads = queries.reshape(length, local_heads, head_width)
    query_feats = normalized(
        jnp.einsum("thc,hcf->htf", query_heads, f_query, preferred_element_type=jnp.float32)
    )
    offsets = jnp.arange(length)[:, None] + WINDOW - jnp.arange(length + WINDOW)[None, :]
    inside = (offsets >= 0) & (offsets < WINDOW) & present[None, :]
    beyond = (offsets >= WINDOW) & present[None, :]
    scale = 1.0 / math.sqrt(head_width)
    scores = (
        jnp.einsum("thc,kc->htk", query_heads, ext_keys, preferred_element_type=jnp.float32) * scale
    )
    near_w = jnp.where(inside[None], jnp.exp(scores), 0.0)
    far_w = jnp.where(
        beyond[None],
        jnp.einsum("htf,kf->htk", query_feats, ext_feats, preferred_element_type=jnp.float32),
        0.0,
    )
    weights = near_w + far_w
    feats_wide = query_feats.astype(jnp.float32)
    numerator = jnp.einsum(
        "htk,kc->htc", weights, ext_vals.astype(jnp.float32), precision=lax.Precision.HIGHEST
    )
    numerator = numerator + jnp.einsum(
        "htf,fc->htc", feats_wide, matrix, precision=lax.Precision.HIGHEST
    )
    denominator = jnp.sum(weights, axis=-1) + jnp.einsum(
        "htf,f->ht", feats_wide, totals, precision=lax.Precision.HIGHEST
    )
    attn_heads = (numerator / denominator[..., None]).astype(jnp.bfloat16)
    attn_rows = jnp.transpose(attn_heads, (1, 0, 2)).reshape(length, local_heads * head_width)
    all_heads = lax.all_gather(attn_rows, "head", axis=1, tiled=True)
    columns = all_heads
    projected = jnp.dot(
        columns,
        lax.all_gather(w_out, "ctx", axis=0, tiled=True),
        preferred_element_type=jnp.float32,
    )
    return projected.astype(jnp.bfloat16)


def solution(mesh):
    in_specs = (
        P("ctx", None),
        P("ctx", "head"),
        P("ctx", "head"),
        P("head", None, None),
        P(),
        P("ctx", "head"),
    )
    out_specs = P("ctx", "head")
    return jax.shard_map(
        per_device, mesh=mesh, in_specs=in_specs, out_specs=out_specs, check_vma=False
    )
```

profile of v0, /device:TPU:1, one launch (start us, length us, event | category | flops | bytes accessed | tf_op | source)
XLA Modules:
  0.0 402.4 jit_solution(3140013990136511824)
XLA Ops:
  6.5 39.9 %all_gather.27 = bf16[16384,16]{0,1:T(8,128)(2,1)S(1)} all-gather(bf16[512,16]{0,1:T(8,128)(2,1)} %param.10), channel_id=1, replica_groups=mesh['ctx'=32,'head'=16] {'ctx'}, dimensions={0}, use_global_device_ids=true | all-gather | bytes 540672 | tf_op jit(solution)/shard_map/all_gather | solution.py:69
  46.5 5.6 %convolution_convert_fusion.3 = bf16[256,16]{0,1:T(8,128)(2,1)S(1)} fusion(bf16[256,16384]{1,0:T(8,128)(2,1)} %param.8, bf16[16384,16]{0,1:T(8,128)(2,1)S(1)} %all_gather.27), kind=kOutput, calls=%fused_computation.16 | convolution fusion | flops 134221824 | bytes 8921088 | tf_op jit(solution)/shard_map/dot_general | solution.py:67
  52.1 35.5 %all_gather.28 = bf16[256,256]{0,1:T(8,128)(2,1)S(1)} all-gather(bf16[256,16]{0,1:T(8,128)(2,1)S(1)} %convolution_convert_fusion.3), channel_id=1, replica_groups=mesh['ctx'=32,'head'=16] {'head'}, dimensions={1}, use_global_device_ids=true | all-gather | bytes 139264 | tf_op jit(solution)/shard_map/all_gather | solution.py:73
  87.7 2.4 collective-permute-start
  90.1 1.3 collective-permute-done
  94.7 35.3 %all-gather.2 = bf16[32,1,256]{2,1,0:T(2,128)(2,1)S(1)} all-gather(bf16[1,1,256]{2,1,0:T(2,128)(2,1)S(1)} %reshape.161), channel_id=3, replica_groups=mesh['ctx'=32,'head'=16] {'ctx'}, dimensions={0}, use_global_device_ids=true | all-gather | bytes 16896 | tf_op jit(solution)/shard_map/all_gather | solution.py:19
  130.0 41.1 %all-gather.14.cloned.1.call-done = bf16[8192,128]{1,0:T(8,128)(2,1)} async-done(((bf16[256,128]{1,0:T(8,128)(2,1)}), bf16[8192,128]{1,0:T(8,128)(2,1)}) %all-gather.14.cloned.1.call-update) | async-done | bytes 2097168 | tf_op jit(solution)/shard_map/all_gather | solution.py:19
  171.1 30.8 %while.16 = (s32[]{:T(128)}, f32[256,128]{1,0:T(8,128)S(1)}, f32[256]{0:T(256)S(1)}, s32[]{:T(128)}, bf16[32,256,128]{2,1,0:T(8,128)(2,1)}, /*index=5*/bf16[32,256]{1,0:T(8,128)(2,1)S(1)}, s32[]{:T(128)}, s32[]{:T(128)}) while((s32[]{:T(128)}, f32[256,128]{1,0:T(8,128)S(1)}, f32[256]{0:T(256)S(1)}, s32[]{:T(128)}, ...), condition=%wide.region_6.7_spmd.clone, body=%wide.region_5.6_spmd.clone.sunk | while | flops 132100 | bytes 332403 | solution.py:36
  172.1 0.9 add_select_fusion.4
  173.1 0.9 add_select_fusion.4
  174.0 0.9 add_select_fusion.4
  175.0 0.9 add_select_fusion.4
  175.9 0.9 add_select_fusion.4
  176.9 0.9 add_select_fusion.4
  177.9 0.9 add_select_fusion.4
  178.8 0.9 add_select_fusion.4
  179.8 0.9 add_select_fusion.4
  180.8 0.9 add_select_fusion.4
  181.7 0.9 add_select_fusion.4
  186.6 0.9 add_select_fusion.4
  189.4 0.9 add_select_fusion.4
  190.4 0.9 add_select_fusion.4
  191.4 0.9 add_select_fusion.4
  192.3 0.9 add_select_fusion.4
  195.2 0.9 add_select_fusion.4
  198.1 0.9 add_select_fusion.4
  202.0 58.0 %all-gather.8.cloned.1.call-done = bf16[16384,128]{1,0:T(8,128)(2,1)} async-done(((bf16[512,128]{1,0:T(8,128)(2,1)}), bf16[16384,128]{1,0:T(8,128)(2,1)}) %all-gather.8.cloned.1.call-update) | async-done | bytes 4194320 | tf_op jit(solution)/shard_map/all_gather | solution.py:64
  260.0 6.9 %convolution_convert_fusion.2 = bf16[256,128]{1,0:T(8,128)(2,1)S(1)} fusion(bf16[256,16384]{1,0:T(8,128)(2,1)} %param.8, bf16[16384,128]{1,0:T(8,128)(2,1)} %all-gather.8.cloned.1.call-done), kind=kOutput, calls=%fused_computation.15 | convolution fusion | flops 1073774592 | bytes 12648448 | tf_op jit(solution)/shard_map/dot_general | solution.py:62
  268.3 1.2 fusion.6
  269.5 78.3 %all-gather.12.cloned.1.call-done = bf16[2048,1024]{1,0:T(8,128)(2,1)} async-done(((bf16[64,1024]{1,0:T(8,128)(2,1)}), bf16[2048,1024]{1,0:T(8,128)(2,1)}) %all-gather.12.cloned.1.call-update) | async-done | bytes 4194320 | tf_op jit(solution)/shard_map/all_gather | solution.py:122
  347.8 43.5 %all-gather.10.cloned.1.call-done = bf16[256,2048]{1,0:T(8,128)(2,1)} async-done(((bf16[256,128]{1,0:T(8,128)(2,1)}), bf16[256,2048]{1,0:T(8,128)(2,1)}) %all-gather.10.cloned.1.call-update) | async-done | bytes 1048592 | tf_op jit(solution)/shard_map/all_gather | solution.py:118
  391.3 4.6 %convolution_convert_fusion = bf16[256,1024]{1,0:T(8,128)(2,1)} fusion(bf16[256,2048]{1,0:T(8,128)(2,1)} %all-gather.10.cloned.1.call-done, bf16[2048,1024]{1,0:T(8,128)(2,1)} %all-gather.12.cloned.1.call-done), kind=kOutput, calls=%fused_computation.3 | convolution fusion | flops 1074003968 | bytes 5767168 | tf_op jit(solution)/shard_map/dot_general | solution.py:120
  (109 shorter events, 18.2 us)
Async XLA Ops:
  6.5 84.9 %copy-start = (bf16[128,128]{1,0:T(8,128)(2,1)S(1)}, bf16[128,128]{1,0:T(8,128)(2,1)}, u32[]{:S(2)}) copy-start(bf16[128,128]{1,0:T(8,128)(2,1)} %param.12) | copy-start | bytes 98308
  6.5 164.6 %all-gather.14.cloned.1.call-start = ((), (), s32[]{:S(2)}) async-start(), calls=%async_computation.3 | async-start | bytes 2162688 | tf_op jit(solution)/shard_map/all_gather | solution.py:19
  87.7 3.7 collective-permute-start
  93.1 166.9 %all-gather.8.cloned.1.call-start = ((), (), s32[]{:S(2)}) async-start(), calls=%async_computation | async-start | bytes 4325376 | tf_op jit(solution)/shard_map/all_gather | solution.py:64
  93.9 253.9 %all-gather.12.cloned.1.call-start = ((), (), s32[]{:S(2)}) async-start(), calls=%async_computation.2 | async-start | bytes 4325376 | tf_op jit(solution)/shard_map/all_gather | solution.py:122
  94.6 296.7 %all-gather.10.cloned.1.call-start = ((), (), s32[]{:S(2)}) async-start(), calls=%async_computation.1 | async-start | bytes 1114112 | tf_op jit(solution)/shard_map/all_gather | solution.py:118
  202.0 64.9 %copy-start.1 = (bf16[1,128,128]{2,1,0:T(8,128)(2,1)S(1)}, bf16[1,128,128]{2,1,0:T(8,128)(2,1)}, u32[]{:S(2)}) copy-start(bf16[1,128,128]{2,1,0:T(8,128)(2,1)} %param.11) | copy-start | bytes 98308
Sparse Core Ops, SparseCore 0:
  93.2 77.8 all-gather.13
  174.3 85.6 all-gather.7
  263.1 84.6 all-gather.11
  349.7 41.5 all-gather.9
where the time goes:
time: 404 us; the launch traced here: 402 us
  waiting for transfers between devices  224 us (55%)
  blocking collectives  111 us (27%)
  other arithmetic  30.2 us (7%)
  matrix products  21 us (5%)
  between operations  13.3 us (3%)
    all_gather x1, waiting for transfers between devices, per_device(): lax.all_gather(w_out, 'ctx', axis=0, tiled=True)  78.3 us
    all_gather x1, waiting for transfers between devices, per_device(): lax.all_gather(w_query, 'ctx', axis=0, tiled=True)  58 us
    all_gather x1, waiting for transfers between devices, per_device(): all_heads = lax.all_gather(attn_rows, 'head', axis=1, tiled=True)  43.5 us
    all_gather x1, waiting for transfers between devices, prefix(): lax.all_gather(part.astype(kind), axis)  41.1 us
    all_gather x1, blocking collectives, per_device(): lax.all_gather(w_keyval, 'ctx', axis=0, tiled=True)  39.9 us
    all_gather x1, blocking collectives, per_device(): lax.all_gather(pair_sum.astype(jnp.bfloat16), 'head', axis=1, tiled=True)  35.5 us
    all_gather x1, blocking collectives, prefix(): lax.all_gather(part.astype(kind), axis)  35.3 us
    select_n x64, other arithmetic, step(): return jax.tree.map(lambda a, b: jnp.where(reached, a, b), new, before)  29.3 us
  transfers between devices with their start and end apart: 5, of which 5 were waited for; matrix products, arithmetic and copies ran while one was open for 10% of the time, Pallas kernels for 0%

commit v1 on v0

--- a/solution.py
+++ b/solution.py
@@ -5,6 +5,27 @@
 from jax.sharding import PartitionSpec as P
 
 WINDOW = 64
+
+
+def collect(array, axis, dim):
+    size, place, extent = (lax.axis_size(axis), lax.axis_index(axis), array.shape[dim])
+    right = [(i, (i + 1) % size) for i in range(size)]
+    downward = [(i, (i - 1) % size) for i in range(size)]
+    whole = jnp.zeros((*array.shape[:dim], size * extent, *array.shape[dim + 1 :]), array.dtype)
+    whole = lax.dynamic_update_slice_in_dim(whole, array, place * extent, axis=dim)
+    from_left = from_right = array
+    middle = size // 2
+    for step in range(1, middle + 1):
+        from_left = lax.ppermute(from_left, axis, right)
+        whole = lax.dynamic_update_slice_in_dim(
+            whole, from_left, (place - step) % size * extent, axis=dim
+        )
+        if step < size - middle:
+            from_right = lax.ppermute(from_right, axis, downward)
+            whole = lax.dynamic_update_slice_in_dim(
+                whole, from_right, (place + step) % size * extent, axis=dim
+            )
+    return whole
 
 
 def from_behind(array, axis, by):
@@ -115,7 +136,7 @@
     )
     attn_heads = (numerator / denominator[..., None]).astype(jnp.bfloat16)
     attn_rows = jnp.transpose(attn_heads, (1, 0, 2)).reshape(length, local_heads * head_width)
-    all_heads = lax.all_gather(attn_rows, "head", axis=1, tiled=True)
+    all_heads = collect(attn_rows, "head", 1)
     columns = all_heads
     projected = jnp.dot(
         columns,

time: 404 us -> 362 us (0.90)
  waiting for transfers between devices: 224 us -> 154 us
  starting transfers between devices: 2.53 us -> 28.9 us
    all_gather x1 -> x0, waiting for transfers between devices: 43.5 us -> none  [per_device(): all_heads = lax.all_gather(attn_rows, 'head', axis=1, tiled=True)]
    all_gather x1, waiting for transfers between devices: 78.3 us -> 40.5 us  [per_device(): lax.all_gather(w_out, 'ctx', axis=0, tiled=True)]
    ppermute x0 -> x15, starting transfers between devices: none -> 26.4 us  [the longest x7 14.9 us: collect(): from_right = lax.ppermute(from_right, axis, downward)]
    ppermute x0 -> x15, waiting for transfers between devices: none -> 11.4 us  [the longest x8 8.4 us: collect(): from_left = lax.ppermute(from_left, axis, right)]
  transfers between devices with their start and end apart: 5 -> 19, of which waited for: 5 -> 16; matrix products, arithmetic and copies ran while one was open for 10% -> 11% of each run, Pallas kernels for 0% -> 0%
where the time goes in v1:
time: 362 us; the launch traced here: 359 us
  waiting for transfers between devices  154 us (43%)
  blocking collectives  111 us (31%)
  other arithmetic  30.1 us (8%)
  starting transfers between devices  28.9 us (8%)
  matrix products  20.1 us (6%)
  between operations  13.4 us (4%)
    all_gather x1, waiting for transfers between devices, per_device(): lax.all_gather(w_query, 'ctx', axis=0, tiled=True)  58 us
    all_gather x1, waiting for transfers between devices, prefix(): lax.all_gather(part.astype(kind), axis)  41.1 us
    all_gather x1, waiting for transfers between devices, per_device(): lax.all_gather(w_out, 'ctx', axis=0, tiled=True)  40.5 us
    all_gather x1, blocking collectives, per_device(): lax.all_gather(w_keyval, 'ctx', axis=0, tiled=True)  39.9 us
    all_gather x1, blocking collectives, per_device(): lax.all_gather(pair_sum.astype(jnp.bfloat16), 'head', axis=1, tiled=True)  35.5 us
    all_gather x1, blocking collectives, prefix(): lax.all_gather(part.astype(kind), axis)  35.3 us
    select_n x64, other arithmetic, step(): return jax.tree.map(lambda a, b: jnp.where(reached, a, b), new, before)  29.3 us
    ppermute x7, starting transfers between devices, collect(): from_right = lax.ppermute(from_right, axis, downward)  14.9 us
  transfers between devices with their start and end apart: 19, of which 16 were waited for; matrix products, arithmetic and copies ran while one was open for 11% of the time, Pallas kernels for 0%

profile of v1, /device:TPU:1, one launch (start us, length us, event | category | flops | bytes accessed | tf_op | source)
XLA Modules:
  0.0 358.6 jit_solution(5445764282447821433)
XLA Ops:
  6.5 39.9 %all_gather.24 = bf16[16384,16]{0,1:T(8,128)(2,1)S(1)} all-gather(bf16[512,16]{0,1:T(8,128)(2,1)} %param.10), channel_id=1, replica_groups=mesh['ctx'=32,'head'=16] {'ctx'}, dimensions={0}, use_global_device_ids=true | all-gather | bytes 540672 | tf_op jit(solution)/shard_map/all_gather | solution.py:90
  46.5 5.6 %convolution_convert_fusion.3 = bf16[256,16]{0,1:T(8,128)(2,1)S(1)} fusion(bf16[256,16384]{1,0:T(8,128)(2,1)} %param.8, bf16[16384,16]{0,1:T(8,128)(2,1)S(1)} %all_gather.24), kind=kOutput, calls=%fused_computation.16 | convolution fusion | flops 134221824 | bytes 8921088 | tf_op jit(solution)/shard_map/dot_general | solution.py:88
  52.1 35.5 %all_gather.25 = bf16[256,256]{0,1:T(8,128)(2,1)S(1)} all-gather(bf16[256,16]{0,1:T(8,128)(2,1)S(1)} %convolution_convert_fusion.3), channel_id=1, replica_groups=mesh['ctx'=32,'head'=16] {'head'}, dimensions={1}, use_global_device_ids=true | all-gather | bytes 139264 | tf_op jit(solution)/shard_map/all_gather | solution.py:94
  87.7 2.4 collective-permute-start
  90.1 1.3 collective-permute-done
  94.7 35.3 %all-gather.2 = bf16[32,1,256]{2,1,0:T(2,128)(2,1)S(1)} all-gather(bf16[1,1,256]{2,1,0:T(2,128)(2,1)S(1)} %reshape.161), channel_id=3, replica_groups=mesh['ctx'=32,'head'=16] {'ctx'}, dimensions={0}, use_global_device_ids=true | all-gather | bytes 16896 | tf_op jit(solution)/shard_map/all_gather | solution.py:40
  130.0 41.1 %all-gather.11.cloned.1.call-done = bf16[8192,128]{1,0:T(8,128)(2,1)} async-done(((bf16[256,128]{1,0:T(8,128)(2,1)}), bf16[8192,128]{1,0:T(8,128)(2,1)}) %all-gather.11.cloned.1.call-update) | async-done | bytes 2097168 | tf_op jit(solution)/shard_map/all_gather | solution.py:40
  171.1 30.8 %while.16 = (s32[]{:T(128)}, f32[256,128]{1,0:T(8,128)S(1)}, f32[256]{0:T(256)S(1)}, s32[]{:T(128)}, bf16[32,256,128]{2,1,0:T(8,128)(2,1)}, /*index=5*/bf16[32,256]{1,0:T(8,128)(2,1)S(1)}, s32[]{:T(128)}, s32[]{:T(128)}) while((s32[]{:T(128)}, f32[256,128]{1,0:T(8,128)S(1)}, f32[256]{0:T(256)S(1)}, s32[]{:T(128)}, ...), condition=%wide.region_6.7_spmd.clone, body=%wide.region_5.6_spmd.clone.sunk | while | flops 132100 | bytes 332403 | solution.py:57
  172.1 0.9 add_select_fusion.4
  173.1 0.9 add_select_fusion.4
  174.0 0.9 add_select_fusion.4
  175.0 0.9 add_select_fusion.4
  175.9 0.9 add_select_fusion.4
  189.4 0.9 add_select_fusion.4
  190.4 0.9 add_select_fusion.4
  191.4 0.9 add_select_fusion.4
  199.1 0.9 add_select_fusion.4
  201.9 58.0 %all-gather.7.cloned.1.call-done = bf16[16384,128]{1,0:T(8,128)(2,1)} async-done(((bf16[512,128]{1,0:T(8,128)(2,1)}), bf16[16384,128]{1,0:T(8,128)(2,1)}) %all-gather.7.cloned.1.call-update) | async-done | bytes 4194320 | tf_op jit(solution)/shard_map/all_gather | solution.py:85
  260.0 6.9 %convolution_convert_fusion.2 = bf16[256,128]{1,0:T(8,128)(2,1)S(1)} fusion(bf16[256,16384]{1,0:T(8,128)(2,1)} %param.8, bf16[16384,128]{1,0:T(8,128)(2,1)} %all-gather.7.cloned.1.call-done), kind=kOutput, calls=%fused_computation.15 | convolution fusion | flops 1073774592 | bytes 12648448 | tf_op jit(solution)/shard_map/dot_general | solution.py:83
  269.0 4.4 %collective-permute-start.1 = (bf16[256,128]{1,0:T(8,128)(2,1)S(1)}, bf16[256,128]{1,0:T(8,128)(2,1)S(1)}, u32[]{:S(2)}, u32[]{:S(2)}) collective-permute-start(bf16[256,128]{1,0:T(8,128)(2,1)S(1)} %get-tuple-element.163), channel_id=1, source_target_pairs={{0,1},{1,2},{2,3},{3,4},{4,5},{5,6},{6,7},{7,8},{8,9},{9,10},{10,1... | collective-permute-start | bytes 196616 | tf_op jit(solution)/shard_map/ppermute | solution.py:19
  273.5 1.3 collective-permute-done.1
  274.8 2.4 collective-permute-start.3
  277.2 1.3 collective-permute-done.3
  278.5 2.4 collective-permute-start.5
  282.8 1.8 collective-permute-start.7
  284.8 2.1 collective-permute-start.8
  288.6 3.5 collective-permute-start.10
  293.0 4.4 %collective-permute-start.12 = (bf16[256,128]{1,0:T(8,128)(2,1)S(1)}, bf16[256,128]{1,0:T(8,128)(2,1)S(1)}, u32[]{:S(2)}, u32[]{:S(2)}) collective-permute-start(bf16[256,128]{1,0:T(8,128)(2,1)S(1)} %collective-permute-done.10), channel_id=1, source_target_pairs={{0,15},{1,0},{2,1},{3,2},{4,3},{5,4},{6,5},{7,6},{8,7},{9,8},{10,9... | collective-permute-start | bytes 196616 | tf_op jit(solution)/shard_map/ppermute | solution.py:24
  298.3 4.0 %collective-permute-start.14 = (bf16[256,128]{1,0:T(8,128)(2,1)S(1)}, bf16[256,128]{1,0:T(8,128)(2,1)S(1)}, u32[]{:S(2)}, u32[]{:S(2)}) collective-permute-start(bf16[256,128]{1,0:T(8,128)(2,1)S(1)} %collective-permute-done.12), channel_id=1, source_target_pairs={{0,15},{1,0},{2,1},{3,2},{4,3},{5,4},{6,5},{7,6},{8,7},{9,8},{10,9... | collective-permute-start | bytes 196616 | tf_op jit(solution)/shard_map/ppermute | solution.py:24
  303.3 4.0 %collective-permute-done.15 = bf16[256,128]{1,0:T(8,128)(2,1)S(1)} collective-permute-done((bf16[256,128]{1,0:T(8,128)(2,1)S(1)}, bf16[256,128]{1,0:T(8,128)(2,1)S(1)}, u32[]{:S(2)}, u32[]{:S(2)}) %collective-permute-start.15) | collective-permute-done | bytes 65568 | tf_op jit(solution)/shard_map/ppermute | solution.py:19
  307.3 40.5 %all-gather.9.cloned.1.call-done = bf16[2048,1024]{1,0:T(8,128)(2,1)} async-done(((bf16[64,1024]{1,0:T(8,128)(2,1)}), bf16[2048,1024]{1,0:T(8,128)(2,1)}) %all-gather.9.cloned.1.call-update) | async-done | bytes 4194320 | tf_op jit(solution)/shard_map/all_gather | solution.py:143
  347.8 4.2 %convolution_convert_fusion = bf16[256,1024]{1,0:T(8,128)(2,1)} fusion(bf16[256,2048]{1,0:T(8,128)(2,1)S(1)} %constant_dynamic-update-slice_fusion, bf16[2048,1024]{1,0:T(8,128)(2,1)} %all-gather.9.cloned.1.call-done), kind=kOutput, calls=%fused_computation.3 | convolution fusion | flops 1074003968 | bytes 5767168 | tf_op jit(solution)/shard_map/dot_general | solution.py:141
  (152 shorter events, 33.6 us)
Async XLA Ops:
  6.5 84.9 %copy-start = (bf16[128,128]{1,0:T(8,128)(2,1)S(1)}, bf16[128,128]{1,0:T(8,128)(2,1)}, u32[]{:S(2)}) copy-start(bf16[128,128]{1,0:T(8,128)(2,1)} %param.12) | copy-start | bytes 98308
  6.5 164.6 %all-gather.11.cloned.1.call-start = ((), (), s32[]{:S(2)}) async-start(), calls=%async_computation.2 | async-start | bytes 2162688 | tf_op jit(solution)/shard_map/all_gather | solution.py:40
  87.7 3.7 %collective-permute-start = (bf16[64,256]{0,1:T(8,128)(2,1)S(1)}, bf16[64,256]{0,1:T(8,128)(2,1)S(1)}, u32[]{:S(2)}, u32[]{:S(2)}) collective-permute-start(bf16[64,256]{0,1:T(8,128)(2,1)S(1)} %slice.21), channel_id=1, source_target_pairs={{0,16},{16,32},{32,48},{48,64},{64,80},{80,96},{96,112},{112,128},... | collective-permute-start | bytes 98312 | tf_op jit(solution)/shard_map/ppermute | solution.py:34
  93.1 166.9 %all-gather.7.cloned.1.call-start = ((), (), s32[]{:S(2)}) async-start(), calls=%async_computation | async-start | bytes 4325376 | tf_op jit(solution)/shard_map/all_gather | solution.py:85
  93.9 253.9 %all-gather.9.cloned.1.call-start = ((), (), s32[]{:S(2)}) async-start(), calls=%async_computation.1 | async-start | bytes 4325376 | tf_op jit(solution)/shard_map/all_gather | solution.py:143
  201.9 64.9 %copy-start.1 = (bf16[1,128,128]{2,1,0:T(8,128)(2,1)S(1)}, bf16[1,128,128]{2,1,0:T(8,128)(2,1)}, u32[]{:S(2)}) copy-start(bf16[1,128,128]{2,1,0:T(8,128)(2,1)} %param.11) | copy-start | bytes 98308
  269.0 5.8 %collective-permute-start.1 = (bf16[256,128]{1,0:T(8,128)(2,1)S(1)}, bf16[256,128]{1,0:T(8,128)(2,1)S(1)}, u32[]{:S(2)}, u32[]{:S(2)}) collective-permute-start(bf16[256,128]{1,0:T(8,128)(2,1)S(1)} %get-tuple-element.163), channel_id=1, source_target_pairs={{0,1},{1,2},{2,3},{3,4},{4,5},{5,6},{6,7},{7,8},{8,9},{9,10},{10,1... | collective-permute-start | bytes 196616 | tf_op jit(solution)/shard_map/ppermute | solution.py:19
  273.5 3.7 %collective-permute-start.2 = (bf16[256,128]{1,0:T(8,128)(2,1)S(1)}, bf16[256,128]{1,0:T(8,128)(2,1)S(1)}, u32[]{:S(2)}, u32[]{:S(2)}) collective-permute-start(bf16[256,128]{1,0:T(8,128)(2,1)S(1)} %get-tuple-element.163), channel_id=1, source_target_pairs={{0,15},{1,0},{2,1},{3,2},{4,3},{5,4},{6,5},{7,6},{8,7},{9,8},{10,9... | collective-permute-start | bytes 196616 | tf_op jit(solution)/shard_map/ppermute | solution.py:24
  274.8 3.7 %collective-permute-start.3 = (bf16[256,128]{1,0:T(8,128)(2,1)S(1)}, bf16[256,128]{1,0:T(8,128)(2,1)S(1)}, u32[]{:S(2)}, u32[]{:S(2)}) collective-permute-start(bf16[256,128]{1,0:T(8,128)(2,1)S(1)} %collective-permute-done.1), channel_id=1, source_target_pairs={{0,1},{1,2},{2,3},{3,4},{4,5},{5,6},{6,7},{7,8},{8,9},{9,10},{10,1... | collective-permute-start | bytes 196616 | tf_op jit(solution)/shard_map/ppermute | solution.py:19
  277.2 4.0 %collective-permute-start.4 = (bf16[256,128]{1,0:T(8,128)(2,1)S(1)}, bf16[256,128]{1,0:T(8,128)(2,1)S(1)}, u32[]{:S(2)}, u32[]{:S(2)}) collective-permute-start(bf16[256,128]{1,0:T(8,128)(2,1)S(1)} %collective-permute-done.2), channel_id=1, source_target_pairs={{0,15},{1,0},{2,1},{3,2},{4,3},{5,4},{6,5},{7,6},{8,7},{9,8},{10,9... | collective-permute-start | bytes 196616 | tf_op jit(solution)/shard_map/ppermute | solution.py:24
  278.5 4.3 %collective-permute-start.5 = (bf16[256,128]{1,0:T(8,128)(2,1)S(1)}, bf16[256,128]{1,0:T(8,128)(2,1)S(1)}, u32[]{:S(2)}, u32[]{:S(2)}) collective-permute-start(bf16[256,128]{1,0:T(8,128)(2,1)S(1)} %collective-permute-done.3), channel_id=1, source_target_pairs={{0,1},{1,2},{2,3},{3,4},{4,5},{5,6},{6,7},{7,8},{8,9},{9,10},{10,1... | collective-permute-start | bytes 196616 | tf_op jit(solution)/shard_map/ppermute | solution.py:19
  281.1 3.7 %collective-permute-start.6 = (bf16[256,128]{1,0:T(8,128)(2,1)S(1)}, bf16[256,128]{1,0:T(8,128)(2,1)S(1)}, u32[]{:S(2)}, u32[]{:S(2)}) collective-permute-start(bf16[256,128]{1,0:T(8,128)(2,1)S(1)} %collective-permute-done.4), channel_id=1, source_target_pairs={{0,15},{1,0},{2,1},{3,2},{4,3},{5,4},{6,5},{7,6},{8,7},{9,8},{10,9... | collective-permute-start | bytes 196616 | tf_op jit(solution)/shard_map/ppermute | solution.py:24
  282.8 4.9 %collective-permute-start.7 = (bf16[256,128]{1,0:T(8,128)(2,1)S(1)}, bf16[256,128]{1,0:T(8,128)(2,1)S(1)}, u32[]{:S(2)}, u32[]{:S(2)}) collective-permute-start(bf16[256,128]{1,0:T(8,128)(2,1)S(1)} %collective-permute-done.5), channel_id=1, source_target_pairs={{0,1},{1,2},{2,3},{3,4},{4,5},{5,6},{6,7},{7,8},{8,9},{9,10},{10,1... | collective-permute-start | bytes 196616 | tf_op jit(solution)/shard_map/ppermute | solution.py:19
  284.8 3.8 %collective-permute-start.8 = (bf16[256,128]{1,0:T(8,128)(2,1)S(1)}, bf16[256,128]{1,0:T(8,128)(2,1)S(1)}, u32[]{:S(2)}, u32[]{:S(2)}) collective-permute-start(bf16[256,128]{1,0:T(8,128)(2,1)S(1)} %collective-permute-done.6), channel_id=1, source_target_pairs={{0,15},{1,0},{2,1},{3,2},{4,3},{5,4},{6,5},{7,6},{8,7},{9,8},{10,9... | collective-permute-start | bytes 196616 | tf_op jit(solution)/shard_map/ppermute | solution.py:24
  287.7 4.9 %collective-permute-start.9 = (bf16[256,128]{1,0:T(8,128)(2,1)S(1)}, bf16[256,128]{1,0:T(8,128)(2,1)S(1)}, u32[]{:S(2)}, u32[]{:S(2)}) collective-permute-start(bf16[256,128]{1,0:T(8,128)(2,1)S(1)} %collective-permute-done.7), channel_id=1, source_target_pairs={{0,1},{1,2},{2,3},{3,4},{4,5},{5,6},{6,7},{7,8},{8,9},{9,10},{10,1... | collective-permute-start | bytes 196616 | tf_op jit(solution)/shard_map/ppermute | solution.py:19
  288.6 4.4 %collective-permute-start.10 = (bf16[256,128]{1,0:T(8,128)(2,1)S(1)}, bf16[256,128]{1,0:T(8,128)(2,1)S(1)}, u32[]{:S(2)}, u32[]{:S(2)}) collective-permute-start(bf16[256,128]{1,0:T(8,128)(2,1)S(1)} %collective-permute-done.8), channel_id=1, source_target_pairs={{0,15},{1,0},{2,1},{3,2},{4,3},{5,4},{6,5},{7,6},{8,7},{9,8},{10,9... | collective-permute-start | bytes 196616 | tf_op jit(solution)/shard_map/ppermute | solution.py:24
  292.6 4.9 %collective-permute-start.11 = (bf16[256,128]{1,0:T(8,128)(2,1)S(1)}, bf16[256,128]{1,0:T(8,128)(2,1)S(1)}, u32[]{:S(2)}, u32[]{:S(2)}) collective-permute-start(bf16[256,128]{1,0:T(8,128)(2,1)S(1)} %collective-permute-done.9), channel_id=1, source_target_pairs={{0,1},{1,2},{2,3},{3,4},{4,5},{5,6},{6,7},{7,8},{8,9},{9,10},{10,1... | collective-permute-start | bytes 196616 | tf_op jit(solution)/shard_map/ppermute | solution.py:19
  293.0 5.3 %collective-permute-start.12 = (bf16[256,128]{1,0:T(8,128)(2,1)S(1)}, bf16[256,128]{1,0:T(8,128)(2,1)S(1)}, u32[]{:S(2)}, u32[]{:S(2)}) collective-permute-start(bf16[256,128]{1,0:T(8,128)(2,1)S(1)} %collective-permute-done.10), channel_id=1, source_target_pairs={{0,15},{1,0},{2,1},{3,2},{4,3},{5,4},{6,5},{7,6},{8,7},{9,8},{10,9... | collective-permute-start | bytes 196616 | tf_op jit(solution)/shard_map/ppermute | solution.py:24
  297.5 4.9 %collective-permute-start.13 = (bf16[256,128]{1,0:T(8,128)(2,1)S(1)}, bf16[256,128]{1,0:T(8,128)(2,1)S(1)}, u32[]{:S(2)}, u32[]{:S(2)}) collective-permute-start(bf16[256,128]{1,0:T(8,128)(2,1)S(1)} %collective-permute-done.11), channel_id=1, source_target_pairs={{0,1},{1,2},{2,3},{3,4},{4,5},{5,6},{6,7},{7,8},{8,9},{9,10},{10,1... | collective-permute-start | bytes 196616 | tf_op jit(solution)/shard_map/ppermute | solution.py:19
  298.3 4.9 %collective-permute-start.14 = (bf16[256,128]{1,0:T(8,128)(2,1)S(1)}, bf16[256,128]{1,0:T(8,128)(2,1)S(1)}, u32[]{:S(2)}, u32[]{:S(2)}) collective-permute-start(bf16[256,128]{1,0:T(8,128)(2,1)S(1)} %collective-permute-done.12), channel_id=1, source_target_pairs={{0,15},{1,0},{2,1},{3,2},{4,3},{5,4},{6,5},{7,6},{8,7},{9,8},{10,9... | collective-permute-start | bytes 196616 | tf_op jit(solution)/shard_map/ppermute | solution.py:24
  302.4 4.9 %collective-permute-start.15 = (bf16[256,128]{1,0:T(8,128)(2,1)S(1)}, bf16[256,128]{1,0:T(8,128)(2,1)S(1)}, u32[]{:S(2)}, u32[]{:S(2)}) collective-permute-start(bf16[256,128]{1,0:T(8,128)(2,1)S(1)} %collective-permute-done.13), channel_id=1, source_target_pairs={{0,1},{1,2},{2,3},{3,4},{4,5},{5,6},{6,7},{7,8},{8,9},{9,10},{10,1... | collective-permute-start | bytes 196616 | tf_op jit(solution)/shard_map/ppermute | solution.py:19
Sparse Core Ops, SparseCore 0:
  93.2 77.8 all-gather.10
  174.3 85.6 all-gather.6
  263.1 84.6 all-gather.8
